TPU v7x, 32 devices: a whole 2x2x4 slice. The times are simulated.
32 devices in a mesh: blk: 8 (over y, x, core), lines: 4 (over z).
Axes of the slice: x: 2, y: 2, z: 4, core: 2. Of those that a mesh axis runs over, the one named last changes fastest.
Arguments:
- velocity: float32 [3, 12288, 1024], P(None, 'lines', 'blk'), may hold values from -6 to 6
- metric: float32 [1024], P('blk'), may hold values from 0.5 to 2
Outputs:
- derivs: float32 [3, 12288, 1024], P(None, 'lines', 'blk')
- profile: float32 [1024], P('blk')
All inputs are finite; a program needn't handle non-finite values.
Results may differ from a plain program's by a relative error of at most 0.00007.
Values sent between devices are 32-bit elements; how exact they have to be, the bound alone decides.
No kernel may reach another device: no remote copies, remote signals or barrier semaphores. Data moves between devices by JAX's collectives and lax.ppermute only.
A program may use at most 128 MiB of HBM per device.

v0:
```python
import jax
import jax.numpy as jnp
from jax import lax
from jax.sharding import PartitionSpec as P

ALPHA = 1.0 / 3.0
COEF_A = 7.0 / 9.0
COEF_B = 1.0 / 36.0


def block_inverse(width):
    counter = jnp.arange(width, dtype=jnp.int32) + 1
    product = counter[:, None] * counter[None, :] % (2 * (width + 1))
    angles = jnp.pi / (width + 1.0)
    sines = jnp.sqrt(2.0 / (width + 1.0)) * jnp.sin(angles * product.astype(jnp.float32))
    eigen = 1.0 + 2.0 * ALPHA * jnp.cos(angles * counter.astype(jnp.float32))
    return jnp.dot(sines / eigen[None, :], sines, precision=lax.Precision.HIGHEST)


def solve_rows(source, inverse):
    shape = source.shape
    flat = jnp.dot(source.reshape(-1, shape[-1]), inverse, precision=lax.Precision.HIGHEST)
    return flat.reshape(shape)


def interface(first_own, last_own, last_left, first_right, couple):
    factor = 1.0 / (1.0 - couple * couple)
    last_prev = (last_left - couple * first_own) * factor
    last_here = (last_own - couple * first_right) * factor
    first_next = first_right - couple * last_here
    return (last_prev, first_next)


def correct(partial_value, inverse, last_prev, first_next):
    width = inverse.shape[0]
    return partial_value - ALPHA * (
        last_prev[..., None] * inverse[:, 0] + first_next[..., None] * inverse[:, width - 1]
    )


def local(velocity, metric):
    width = velocity.shape[2]
    inverse = block_inverse(width)
    couple = ALPHA * inverse[0, 0]
    lines_block = lax.all_to_all(velocity, "blk", split_axis=1, concat_axis=2, tiled=True)
    count = lines_block.shape[-1]
    source = COEF_A * (jnp.roll(lines_block, -1, -1) - jnp.roll(lines_block, 1, -1)) + COEF_B * (
        jnp.roll(lines_block, -2, -1) - jnp.roll(lines_block, 2, -1)
    )
    blocks = source.reshape(lines_block.shape[0], lines_block.shape[1], count // width, width)
    partial_value = solve_rows(blocks, inverse)
    first_own = partial_value[..., 0]
    last_own = partial_value[..., width - 1]
    last_prev, first_next = interface(
        first_own, last_own, jnp.roll(last_own, 1, 2), jnp.roll(first_own, -1, 2), couple
    )
    whole = correct(partial_value, inverse, last_prev, first_next).reshape(lines_block.shape)
    solved = lax.all_to_all(whole, "blk", split_axis=2, concat_axis=1, tiled=True)
    derivs = solved * metric
    squares = jnp.sum(derivs * derivs, axis=(0, 1))
    total = lax.psum(squares, "lines")
    profile = total / (velocity.shape[1] * lax.axis_size("lines"))
    return (derivs, profile)


def solution(mesh):
    in_specs = (P(None, "lines", "blk"), P("blk"))
    out_specs = (P(None, "lines", "blk"), P("blk"))
    return jax.shard_map(local, mesh=mesh, in_specs=in_specs, out_specs=out_specs, check_vma=False)
```

profile of v0, /device:TPU:0, one launch (start us, length us, event | category | flops | bytes accessed | tf_op | source)
XLA Modules:
  0.0 224.0 jit_solution(313442755634897913)
XLA Ops:
  0.6 8.7 %copy.19 = f32[3,3072,128]{2,0,1:T(4,128)} copy(f32[3,3072,128]{2,1,0:T(8,128)} %param.2) | data formatting | bytes 9437184 | tf_op args[0]
  9.3 5.2 %all-to-all-start = ((f32[3,3072,128]{2,0,1:T(4,128)}), f32[3,3072,128]{2,0,1:T(4,128)}, u32[]{:S(2)}, u32[]{:S(2)}) async-start(f32[3,3072,128]{2,0,1:T(4,128)} %copy.19), calls=%async_computation | async-start | bytes 12582912 | tf_op jit(solution)/shard_map/all_to_all | solution.py:45
  14.6 0.9 fusion.3
  15.4 0.5 slice.91
  17.9 68.4 %all-to-all-done = f32[3,3072,128]{2,0,1:T(4,128)} async-done(((f32[3,3072,128]{2,0,1:T(4,128)}), f32[3,3072,128]{2,0,1:T(4,128)}, u32[]{:S(2)}, u32[]{:S(2)}) %all-to-all-start) | async-done | bytes 4718624 | tf_op jit(solution)/shard_map/all_to_all | solution.py:45
  86.3 5.3 %copy.20 = f32[3,3072,128]{2,1,0:T(8,128)} copy(f32[3,3072,128]{2,0,1:T(4,128)} %all-to-all-done) | data formatting | bytes 9437184 | tf_op jit(solution)/shard_map/all_to_all | solution.py:45
  91.6 6.1 %copy.21 = f32[3,384,8,128]{1,3,2,0:T(8,128)} copy(f32[3,384,8,128]{3,1,2,0:T(8,128)} %bitcast.50) | data formatting | bytes 9437184 | tf_op jit(solution)/shard_map/all_to_all | solution.py:45
  97.7 0.0 copy-start
  97.7 4.5 %fusion.33 = (f32[3,384,1023]{1,2,0:T(8,128)S(1)}, f32[3,384,1023]{1,2,0:T(8,128)S(1)}) fusion(f32[3,384,1024]{1,2,0:T(8,128)} %bitcast.42), kind=kLoop, calls=%fused_computation.53 | loop fusion | bytes 18855936 | tf_op jit(solution)/shard_map/jit(_roll_static)/slice | solution.py:47
  102.2 0.6 copy-done
  102.8 2.8 %fusion.31 = (f32[3,384,1022]{1,2,0:T(8,128)S(1)}, f32[3,384,1022]{1,2,0:T(8,128)}) fusion(f32[3,384,1024]{1,2,0:T(8,128)S(1)} %bitcast.43), kind=kLoop, calls=%fused_computation.51 | loop fusion | bytes 18837504 | tf_op jit(solution)/shard_map/jit(_roll_static)/slice | solution.py:48
  105.6 6.7 %fusion.1 = f32[3,384,1024]{1,2,0:T(8,128)S(1)} fusion(f32[3,384,1]{1,2,0:T(1,128)S(1)} %get-tuple-element.9, f32[3,384,1023]{1,2,0:T(8,128)S(1)} %get-tuple-element.11, f32[3,384,1023]{1,2,0:T(8,128)S(1)} %get-tuple-element.10, f32[3,384,1]{1,2,0:T(1,128)S(1)} %get-tuple-element.8, f32[3,384,2]{1,2,0:T(2,128)S(1)} %get-tuple-element.5, ...), kind=kLoop, calls=%fused_computation.3 | loop fusion | flops 10616832 | bytes 23592960 | tf_op jit(solution)/shard_map/add | solution.py:47
  112.3 4.7 %fusion.10 = f32[3,384,8,128]{1,3,2,0:T(8,128)S(1)} fusion(f32[3,384,8,128]{1,3,2,0:T(8,128)S(1)} %bitcast.48, f32[128,128]{0,1:T(8,128)S(1)} %fusion.3), kind=kOutput, calls=%fused_computation.15 | convolution fusion | flops 1811939328 | bytes 9502720 | tf_op jit(solution)/shard_map/dot_general | solution.py:22
  117.1 0.1 fusion.29
  117.3 1.0 multiply_subtract_fusion
  118.3 3.2 %copy.26 = f32[3,384,1024]{1,0,2:T(4,128)S(1)} copy(f32[3,384,1024]{1,2,0:T(8,128)S(1)} %bitcast.49) | data formatting | bytes 9437184 | tf_op jit(solution)/shard_map/reshape | solution.py:57
  121.5 74.9 %all_to_all.36 = f32[3,384,1024]{1,0,2:T(4,128)} all-to-all(f32[3,384,1024]{1,0,2:T(4,128)S(1)} %copy.26), channel_id=1, replica_groups=mesh['blk'=8,'lines'=4] {'blk'}, dimensions={2} | all-to-all | bytes 9437184 | tf_op jit(solution)/shard_map/all_to_all | solution.py:58
  196.4 0.0 copy-start.2
  196.4 6.9 %copy.27 = f32[3,8,384,128]{3,2,1,0:T(8,128)} copy(f32[3,8,384,128]{2,0,3,1:T(4,128)} %bitcast.46) | data formatting | bytes 9437184 | tf_op jit(solution)/shard_map/all_to_all | solution.py:58
  203.3 0.0 copy-done.2
  203.3 0.0 copy-start.1
  203.3 4.9 %multiply_reduce_fusion = f32[128]{0:T(128)S(1)} fusion(f32[3,8,384,128]{2,0,3,1:T(4,128)} %bitcast.47, f32[128]{0:T(128)S(1)} %copy-done.2), kind=kLoop, calls=%fused_computation | loop fusion | flops 3538816 | bytes 4719616 | tf_op jit(solution)/shard_map/reduce_sum | solution.py:60
  208.3 0.0 copy-done.1
  208.3 2.5 %bitcast_multiply_fusion = f32[3,3072,128]{2,1,0:T(8,128)} fusion(f32[3,8,384,128]{3,2,1,0:T(8,128)S(1)} %copy-done.1, f32[128]{0:T(128)S(1)} %copy-done.2), kind=kLoop, calls=%fused_computation.6 | loop fusion | flops 1179648 | bytes 9437696 | tf_op jit(solution)/shard_map/mul | solution.py:59
  210.8 12.7 %psum.7 = f32[128]{0:T(128)S(1)} all-reduce(f32[128]{0:T(128)S(1)} %multiply_reduce_fusion), channel_id=1, replica_groups=mesh['blk'=8,'lines'=4] {'lines'}, use_global_device_ids=true, to_apply=%region_1.2 | all-reduce | flops 128 | bytes 1024 | tf_op jit(solution)/shard_map/psum | solution.py:61
  223.5 0.5 broadcast_multiply_fusion
  (12 shorter events, 0.1 us)
Async XLA Ops:
  9.3 77.0 %all-to-all-start = ((f32[3,3072,128]{2,0,1:T(4,128)}), f32[3,3072,128]{2,0,1:T(4,128)}, u32[]{:S(2)}, u32[]{:S(2)}) async-start(f32[3,3072,128]{2,0,1:T(4,128)} %copy.19), calls=%async_computation | async-start | bytes 12582912 | tf_op jit(solution)/shard_map/all_to_all | solution.py:45
  97.7 5.1 %copy-start = (f32[3,384,8,128]{1,3,2,0:T(8,128)S(1)}, f32[3,384,8,128]{1,3,2,0:T(8,128)}, u32[]{:S(2)}) copy-start(f32[3,384,8,128]{1,3,2,0:T(8,128)} %copy.21) | copy-start | bytes 14155780
  196.4 6.9 %copy-start.2 = (f32[128]{0:T(128)S(1)}, f32[128]{0:T(128)}, u32[]{:S(2)}) copy-start(f32[128]{0:T(128)} %param.3) | copy-start | bytes 1540
  203.3 5.0 %copy-start.1 = (f32[3,8,384,128]{3,2,1,0:T(8,128)S(1)}, f32[3,8,384,128]{3,2,1,0:T(8,128)}, u32[]{:S(2)}) copy-start(f32[3,8,384,128]{3,2,1,0:T(8,128)} %copy.27) | copy-start | bytes 14155780
where the time goes:
time: 225 us; the launch traced here: 224 us
  blocking collectives  87.6 us (39%)
  waiting for transfers between devices  68.4 us (30%)
  local copies, waits for them, and re-layouts  38.7 us (17%)
  other arithmetic  15.8 us (7%)
  matrix products  5.58 us (2%)
  starting transfers between devices  5.17 us (2%)
  between operations  2.74 us (1%)
    all_to_all x1, blocking collectives, local(): lax.all_to_all(whole, 'blk', split_axis=2, concat_axis=1, tiled=True)  74.9 us
    all_to_all x1, waiting for transfers between devices, local(): lax.all_to_all(velocity, 'blk', split_axis=1, concat_axis=2, tiled=True)  68.4 us
    psum x1, blocking collectives, local(): total = lax.psum(squares, 'lines')  12.7 us
    all_to_all x2, local copies, waits for them, and re-layouts, local(): lax.all_to_all(velocity, 'blk', split_axis=1, concat_axis=2, tiled=True)  11.3 us
    unnamed x8, local copies, waits for them, and re-layouts  9.3 us
    all_to_all x1, local copies, waits for them, and re-layouts, local(): lax.all_to_all(whole, 'blk', split_axis=2, concat_axis=1, tiled=True)  6.91 us
    add x1, other arithmetic, local(): COEF_A * (jnp.roll(lines_block, -1, -1) - jnp.roll(lines_block, 1, -1))  6.72 us
    all_to_all x1, starting transfers between devices, local(): lax.all_to_all(velocity, 'blk', split_axis=1, concat_axis=2, tiled=True)  5.17 us
  transfers between devices with their start and end apart: 1, of which 1 were waited for; matrix products, arithmetic and copies ran while one was open for 1% of the time, Pallas kernels for 0%

commit v1 on v0

--- a/solution.py
+++ b/solution.py
@@ -42,7 +42,10 @@
     width = velocity.shape[2]
     inverse = block_inverse(width)
     couple = ALPHA * inverse[0, 0]
-    lines_block = lax.all_to_all(velocity, "blk", split_axis=1, concat_axis=2, tiled=True)
+    lines_block = jnp.concatenate(
+        lax.all_to_all(jnp.stack(jnp.split(velocity, lax.axis_size("blk"), axis=1)), "blk", 0, 0),
+        axis=2,
+    )
     count = lines_block.shape[-1]
     source = COEF_A * (jnp.roll(lines_block, -1, -1) - jnp.roll(lines_block, 1, -1)) + COEF_B * (
         jnp.roll(lines_block, -2, -1) - jnp.roll(lines_block, 2, -1)

time: 225 us -> 206 us (0.916)
  waiting for transfers between devices: 68.4 us -> 51.4 us
    all_to_all x1, waiting for transfers between devices: 68.4 us -> 51.4 us  [local(): lax.all_to_all(jnp.stack(jnp.split(velocity, lax.axis_size('blk'), axis=1...]
    all_to_all x2 -> x1, local copies, waits for them, and re-layouts: 11.3 us -> 2.64 us  [local(): lax.all_to_all(jnp.stack(jnp.split(velocity, lax.axis_size('blk'), axis=1...]
    unnamed x8 -> x20, local copies, waits for them, and re-layouts: 9.3 us -> 15.7 us
    slice x2, local copies, waits for them, and re-layouts: 4.52 us -> 0.63 us  [local(): jnp.roll(lines_block, 1, -1)]
    split x0 -> x1, local copies, waits for them, and re-layouts: none -> 3.66 us  [local(): jnp.split(velocity, lax.axis_size('blk'), axis=1)]
where the time goes in v1:
time: 206 us; the launch traced here: 205 us
  blocking collectives  87.6 us (43%)
  waiting for transfers between devices  51.4 us (25%)
  local copies, waits for them, and re-layouts  37 us (18%)
  other arithmetic  15.8 us (8%)
  matrix products  5.58 us (3%)
  starting transfers between devices  5.17 us (3%)
  between operations  2.76 us (1%)
    all_to_all x1, blocking collectives, local(): lax.all_to_all(whole, 'blk', split_axis=2, concat_axis=1, tiled=True)  74.9 us
    all_to_all x1, waiting for transfers between devices, local(): lax.all_to_all(jnp.stack(jnp.split(velocity, lax.axis_size('blk'), axis=1...  51.4 us
    unnamed x20, local copies, waits for them, and re-layouts  15.7 us
    psum x1, blocking collectives, local(): total = lax.psum(squares, 'lines')  12.7 us
    all_to_all x1, local copies, waits for them, and re-layouts, local(): lax.all_to_all(whole, 'blk', split_axis=2, concat_axis=1, tiled=True)  6.91 us
    add x1, other arithmetic, local(): COEF_A * (jnp.roll(lines_block, -1, -1) - jnp.roll(lines_block, 1, -1))  6.72 us
    all_to_all x1, starting transfers between devices, local(): lax.all_to_all(jnp.stack(jnp.split(velocity, lax.axis_size('blk'), axis=1...  5.17 us
    reduce_sum x1, other arithmetic, local(): squares = jnp.sum(derivs * derivs, axis=(0, 1))  4.95 us
  transfers between devices with their start and end apart: 1, of which 1 were waited for; matrix products, arithmetic and copies ran while one was open for 1% of the time, Pallas kernels for 0%

profile of v1, /device:TPU:0, one launch (start us, length us, event | category | flops | bytes accessed | tf_op | source)
XLA Modules:
  0.0 205.4 jit_solution(2516222494657116879)
XLA Ops:
  0.6 3.7 %fusion.34 = (f32[3,384,128]{2,1,0:T(8,128)S(1)}, f32[3,384,128]{2,1,0:T(8,128)S(1)}, f32[3,384,128]{2,1,0:T(8,128)S(1)}, f32[3,384,128]{2,1,0:T(8,128)S(1)}, f3...) fusion(f32[3,3072,128]{2,1,0:T(8,128)} %param.2), kind=kLoop, calls=%fused_computation.62 | loop fusion | bytes 9437184 | tf_op jit(solution)/shard_map/split | solution.py:46
  4.3 2.1 %copy.39 = f32[3,384,128]{1,2,0:T(8,128)} copy(f32[3,384,128]{2,1,0:T(8,128)} %get-tuple-element.19) | data formatting | bytes 1179648
  6.4 1.9 bitcast_dynamic-update-slice_fusion.7
  8.3 2.1 %copy.40 = f32[3,384,128]{1,2,0:T(8,128)} copy(f32[3,384,128]{2,1,0:T(8,128)} %get-tuple-element.18) | data formatting | bytes 1179648
  10.5 1.1 copy.41
  11.5 0.2 copy.42
  11.8 0.2 copy.43
  12.0 0.2 copy.44
  12.2 0.2 copy.45
  12.5 0.2 copy.46
  12.7 1.9 bitcast_dynamic-update-slice_fusion.6
  14.6 1.9 bitcast_dynamic-update-slice_fusion.5
  16.5 0.9 bitcast_dynamic-update-slice_fusion.4
  17.4 0.9 bitcast_dynamic-update-slice_fusion.3
  18.2 0.9 bitcast_dynamic-update-slice_fusion.2
  19.1 0.9 bitcast_dynamic-update-slice_fusion.1
  20.0 0.9 bitcast_dynamic-update-slice_fusion
  20.8 5.2 %all-to-all-start = ((f32[8,3,384,128]{2,3,1,0:T(8,128)}), f32[8,3,384,128]{2,3,1,0:T(8,128)}, u32[]{:S(2)}, u32[]{:S(2)}) async-start(f32[8,3,384,128]{2,3,1,0:T(8,128)} %bitcast_dynamic-update-slice_fusion), calls=%async_computation | async-start | bytes 9437184 | tf_op jit(solution)/shard_map/all_to_all | solution.py:46
  26.0 0.9 fusion.3
  26.9 0.5 slice.91
  29.4 51.4 %all-to-all-done = f32[8,3,384,128]{2,3,1,0:T(8,128)} async-done(((f32[8,3,384,128]{2,3,1,0:T(8,128)}), f32[8,3,384,128]{2,3,1,0:T(8,128)}, u32[]{:S(2)}, u32[]{:S(2)}) %all-to-all-start) | async-done | bytes 4718624 | tf_op jit(solution)/shard_map/all_to_all | solution.py:46
  80.8 2.6 %copy.29 = f32[8,3,384,128]{2,3,0,1:T(8,128)S(1)} copy(f32[8,3,384,128]{2,3,1,0:T(8,128)} %all-to-all-done) | data formatting | bytes 9437184 | tf_op jit(solution)/shard_map/all_to_all | solution.py:46
  83.5 0.6 fusion.33
  84.1 2.8 %fusion.31 = (f32[3,384,1022]{1,2,0:T(8,128)S(1)}, f32[3,384,1022]{1,2,0:T(8,128)}) fusion(f32[3,384,1024]{1,2,0:T(8,128)S(1)} %bitcast.58), kind=kLoop, calls=%fused_computation.59 | loop fusion | bytes 18837504 | tf_op jit(solution)/shard_map/jit(_roll_static)/slice | solution.py:51
  86.9 6.7 %fusion.1 = f32[3,384,1024]{1,2,0:T(8,128)S(1)} fusion(f32[3,384,1]{1,2,0:T(1,128)S(1)} %get-tuple-element.9, f32[3,384,1023]{1,2,0:T(8,128)S(1)} %get-tuple-element.11, f32[3,384,1023]{1,2,0:T(8,128)S(1)} %get-tuple-element.10, f32[3,384,1]{1,2,0:T(1,128)S(1)} %get-tuple-element.8, f32[3,384,2]{1,2,0:T(2,128)S(1)} %get-tuple-element.5, ...), kind=kLoop, calls=%fused_computation.3 | loop fusion | flops 10616832 | bytes 23592960 | tf_op jit(solution)/shard_map/add | solution.py:50
  93.7 4.7 %fusion.10 = f32[3,384,8,128]{1,3,2,0:T(8,128)S(1)} fusion(f32[3,384,8,128]{1,3,2,0:T(8,128)S(1)} %bitcast.63, f32[128,128]{0,1:T(8,128)S(1)} %fusion.3), kind=kOutput, calls=%fused_computation.23 | convolution fusion | flops 1811939328 | bytes 9502720 | tf_op jit(solution)/shard_map/dot_general | solution.py:22
  98.4 0.1 fusion.29
  98.6 1.0 multiply_subtract_fusion
  99.6 3.2 %copy.34 = f32[3,384,1024]{1,0,2:T(4,128)S(1)} copy(f32[3,384,1024]{1,2,0:T(8,128)S(1)} %bitcast.64) | data formatting | bytes 9437184 | tf_op jit(solution)/shard_map/reshape | solution.py:60
  102.9 74.9 %all_to_all.23 = f32[3,384,1024]{1,0,2:T(4,128)} all-to-all(f32[3,384,1024]{1,0,2:T(4,128)S(1)} %copy.34), channel_id=1, replica_groups=mesh['blk'=8,'lines'=4] {'blk'}, dimensions={2} | all-to-all | bytes 9437184 | tf_op jit(solution)/shard_map/all_to_all | solution.py:61
  177.8 0.0 copy-start.1
  177.8 6.9 %copy.35 = f32[3,8,384,128]{3,2,1,0:T(8,128)} copy(f32[3,8,384,128]{2,0,3,1:T(4,128)} %bitcast.61) | data formatting | bytes 9437184 | tf_op jit(solution)/shard_map/all_to_all | solution.py:61
  184.7 0.0 copy-done.1
  184.7 0.0 copy-start
  184.7 4.9 %multiply_reduce_fusion = f32[128]{0:T(128)S(1)} fusion(f32[3,8,384,128]{2,0,3,1:T(4,128)} %bitcast.62, f32[128]{0:T(128)S(1)} %copy-done.1), kind=kLoop, calls=%fused_computation | loop fusion | flops 3538816 | bytes 4719616 | tf_op jit(solution)/shard_map/reduce_sum | solution.py:63
  189.6 0.0 copy-done
  189.6 2.5 %bitcast_multiply_fusion = f32[3,3072,128]{2,1,0:T(8,128)} fusion(f32[3,8,384,128]{3,2,1,0:T(8,128)S(1)} %copy-done, f32[128]{0:T(128)S(1)} %copy-done.1), kind=kLoop, calls=%fused_computation.6 | loop fusion | flops 1179648 | bytes 9437696 | tf_op jit(solution)/shard_map/mul | solution.py:62
  192.1 12.7 %psum.7 = f32[128]{0:T(128)S(1)} all-reduce(f32[128]{0:T(128)S(1)} %multiply_reduce_fusion), channel_id=1, replica_groups=mesh['blk'=8,'lines'=4] {'lines'}, use_global_device_ids=true, to_apply=%region_1.2 | all-reduce | flops 128 | bytes 1024 | tf_op jit(solution)/shard_map/psum | solution.py:64
  204.8 0.5 broadcast_multiply_fusion
  (12 shorter events, 0.1 us)
Async XLA Ops:
  20.8 60.0 %all-to-all-start = ((f32[8,3,384,128]{2,3,1,0:T(8,128)}), f32[8,3,384,128]{2,3,1,0:T(8,128)}, u32[]{:S(2)}, u32[]{:S(2)}) async-start(f32[8,3,384,128]{2,3,1,0:T(8,128)} %bitcast_dynamic-update-slice_fusion), calls=%async_computation | async-start | bytes 9437184 | tf_op jit(solution)/shard_map/all_to_all | solution.py:46
  177.8 6.9 %copy-start.1 = (f32[128]{0:T(128)S(1)}, f32[128]{0:T(128)}, u32[]{:S(2)}) copy-start(f32[128]{0:T(128)} %param.3) | copy-start | bytes 1540
  184.7 5.0 %copy-start = (f32[3,8,384,128]{3,2,1,0:T(8,128)S(1)}, f32[3,8,384,128]{3,2,1,0:T(8,128)}, u32[]{:S(2)}) copy-start(f32[3,8,384,128]{3,2,1,0:T(8,128)} %copy.35) | copy-start | bytes 14155780
